TPU v7x, 32 devices: a whole 2x2x4 slice. The times are simulated.
32 devices in a mesh: beam: 4 (over z), pulse: 4 (over x, core), range: 2 (over y).
Axes of the slice: x: 2, y: 2, z: 4, core: 2. Of those that a mesh axis runs over, the one named last changes fastest.
Arguments:
- signal: bfloat16 [8, 32, 2, 1024], P('beam', 'pulse', None, 'range'), may hold values from -40 to 40, as said below
- replica: bfloat16 [2, 2048], P(None, ('beam', 'pulse')), may hold values from -0.09375 to 0.09375
- guard_cells: int32 [8], P('beam'), may hold values from 1 to 8, as said below
- train_cells: int32 [8], P('beam'), may hold values from 64 to 96, as said below
- scale_index: int32 [8], P('beam'), may hold values from 0 to 15
- offsets: int32 [8], P('beam'), may hold values from 0 to 127, as said below
Outputs:
- compressed: bfloat16 [8, 32, 2, 1024], P('beam', 'pulse', None, 'range')
- test_ratio: float32 [8, 32, 1024], P('beam', 'pulse', 'range')
Inputs may be any that keep to these rules, and one draw needn't show every extreme that they name: `signal`: values stay within the range, with cell-to-cell varying levels. `guard_cells`: some beam has exactly 8 guard cells. `train_cells`: the beam with 8 guard cells has 96 training cells. `offsets`: some beam has the offset 128 - 1.
All inputs are finite; a program needn't handle non-finite values.
Results may differ from a plain program's by a relative error of at most 0.001.
Values may be sent and summed in bfloat16 or wider, within the bound.
A program may use at most 64 MiB of HBM per device.

v0:
```python
import jax
import jax.numpy as jnp
from jax import lax
from jax.sharding import PartitionSpec as P

TILE = 128
OFF_MAX = 128
GUARD_MAX = 8
TRAIN_MAX = 96
EPSILON = 1e-06


def passed_along(array, axis, by):
    devices = lax.axis_size(axis)
    pairs = [(i, i + by) for i in range(devices) if 0 <= i + by < devices]
    return lax.ppermute(array, axis, pairs)


def padded_2(cells, sides, width):
    for axis, dim in sides:
        count = lax.axis_size(axis)
        ends = count - 1
        head = lax.slice_in_dim(cells, 0, width, axis=dim)
        tail = lax.slice_in_dim(cells, cells.shape[dim] - width, cells.shape[dim], axis=dim)
        cells = jnp.concatenate(
            [
                lax.ppermute(tail, axis, [(i, (i + 1) % count) for i in range(ends)]),
                cells,
                lax.ppermute(head, axis, [((i + 1) % count, i) for i in range(ends)]),
            ],
            axis=dim,
        )
    return cells


def panels(whole):
    width = TILE + whole.shape[1]

    def skewed(values):
        padded = jnp.concatenate([values, jnp.zeros((TILE + 1,), values.dtype)])
        flat = jnp.tile(padded, TILE)[: TILE * width]
        return flat.reshape(TILE, width)

    return (skewed(whole[0]), skewed(whole[1]))


def compress(extended, offsets, panel_real, panel_imag, tiles):
    beams, pulses = (extended.shape[0], extended.shape[1])
    width = panel_real.shape[1]
    span = tiles * TILE + width - TILE

    def align(block, start):
        return lax.dynamic_slice_in_dim(block, start, span, 2)

    aligned = jax.vmap(align)(extended, offsets)
    rows = beams * pulses
    group = max(1, min(tiles, 256 // rows))
    while tiles % group:
        group = group - 1
    blocks = tiles // group
    dims = (((1,), (1,)), ((), ()))

    def block_fn(index):
        first = index * (group * TILE)
        windows = jnp.stack(
            [
                lax.dynamic_slice_in_dim(aligned, first + step * TILE, width, 3)
                for step in range(group)
            ]
        )
        real_part = windows[:, :, :, 0, :].reshape(group * rows, width)
        imag_part = windows[:, :, :, 1, :].reshape(group * rows, width)
        out_real = lax.dot_general(
            real_part, panel_real, dims, preferred_element_type=jnp.float32
        ) + lax.dot_general(imag_part, panel_imag, dims, preferred_element_type=jnp.float32)
        out_imag = lax.dot_general(
            imag_part, panel_real, dims, preferred_element_type=jnp.float32
        ) - lax.dot_general(real_part, panel_imag, dims, preferred_element_type=jnp.float32)
        return jnp.stack([out_real, out_imag], axis=1).reshape(group, beams, pulses, 2, TILE)

    outputs = lax.map(block_fn, jnp.arange(blocks, dtype=jnp.int32))
    outputs = outputs.reshape(tiles, beams, pulses, 2, TILE)
    return jnp.transpose(outputs, (1, 2, 3, 0, 4)).reshape(beams, pulses, 2, tiles * TILE)


def cell_power(compressed):
    real_part = compressed[:, :, 0].astype(jnp.float32)
    imag_part = compressed[:, :, 1].astype(jnp.float32)
    return real_part * real_part + imag_part * imag_part


def detect(padded, guard_cells, train_cells, scale_index, first_gate, total_gates):
    margin = GUARD_MAX + TRAIN_MAX
    beams, pulses = (padded.shape[0], padded.shape[1])
    length = padded.shape[2] - 2 * margin
    running = jnp.cumsum(padded, axis=2)
    prefix = jnp.concatenate([jnp.zeros((beams, pulses, 1), jnp.float32), running], axis=2)
    local = jnp.arange(length, dtype=jnp.int32)[None, :]
    guard = guard_cells[:, None]
    train = train_cells[:, None]

    def window(block, start):
        return lax.dynamic_slice_in_dim(block, start, length, 1)

    def pick(starts):
        return jax.vmap(window)(prefix, starts)

    lag = pick(margin - guard_cells) - pick(margin - guard_cells - train_cells)
    lead = pick(margin + guard_cells + train_cells + 1) - pick(margin + guard_cells + 1)
    position = first_gate + local
    count = jnp.clip(position - guard, 0, train) + jnp.clip(
        total_gates - 1 - position - guard, 0, train
    )
    noise = (lag + lead) / count.astype(jnp.float32)[:, None, :]
    factor = jnp.exp2(scale_index.astype(jnp.float32) / 8.0)
    power = padded[:, :, margin : margin + length]
    return power / (factor[:, None, None] * (noise + EPSILON))


def body(signal, replica, guard_cells, train_cells, scale_index, offsets):
    whole = lax.all_gather(replica, ("beam", "pulse"), axis=1, tiled=True)
    panel_real, panel_imag = panels(whole)
    gate_count = signal.shape[3]
    margin = GUARD_MAX + TRAIN_MAX
    needed = whole.shape[1] + OFF_MAX
    limit = min(-(-needed // gate_count), lax.axis_size("range") - 1)
    pieces = [signal]
    for step in range(1, limit + 1):
        keep = min(gate_count, needed - (step - 1) * gate_count)
        pieces.append(passed_along(signal[:, :, :, :keep], "range", -step))
    extended = jnp.concatenate(pieces, axis=3)
    extra = gate_count + needed - extended.shape[3]
    extended = jnp.pad(extended, ((0, 0), (0, 0), (0, 0), (0, extra)))
    compressed = compress(extended, offsets, panel_real, panel_imag, gate_count // TILE).astype(
        jnp.bfloat16
    )
    power = cell_power(compressed)
    padded = padded_2(power, (("range", 2),), margin)
    first_gate = lax.axis_index("range") * gate_count
    total_gates = gate_count * lax.axis_size("range")
    test_ratio = detect(padded, guard_cells, train_cells, scale_index, first_gate, total_gates)
    return (compressed, test_ratio)


def solution(mesh):
    placed = (
        P("beam", "pulse", None, "range"),
        P(None, ("beam", "pulse")),
        P("beam"),
        P("beam"),
        P("beam"),
        P("beam"),
    )
    return jax.shard_map(
        body,
        mesh=mesh,
        in_specs=placed,
        out_specs=(P("beam", "pulse", None, "range"), P("beam", "pulse", "range")),
        check_vma=False,
    )
```

profile of v0, /device:TPU:0, one launch (start us, length us, event | category | flops | bytes accessed | tf_op | source)
XLA Modules:
  0.0 62.5 jit_solution(7068981721563648878)
XLA Ops:
  0.6 1.3 %collective-permute-start = (bf16[2,8,2,512]{3,2,1,0:T(2,128)(2,1)}, bf16[2,8,2,512]{3,2,1,0:T(2,128)(2,1)S(1)}, u32[]{:S(2)}, u32[]{:S(2)}) collective-permute-start(bf16[2,8,2,512]{3,2,1,0:T(2,128)(2,1)} %param.6), channel_id=1, source_target_pairs={{1,0},{3,2},{5,4},{7,6},{9,8},{11,10},{13,12},{15,14},{17,16},{19,... | collective-permute-start | bytes 98312 | tf_op jit(solution)/shard_map/ppermute | solution.py:16
  1.9 0.6 %copy-done.4 = s32[2]{0:T(128)S(1)} copy-done((s32[2]{0:T(128)S(1)}, s32[2]{0:T(128)}, u32[]{:S(2)}) %copy-start.4) | copy-done | bytes 32
  2.6 0.6 %copy-done.3 = bf16[2,128]{1,0:T(2,128)(2,1)S(1)} copy-done((bf16[2,128]{1,0:T(2,128)(2,1)S(1)}, bf16[2,128]{1,0:T(2,128)(2,1)}, u32[]{:S(2)}) %copy-start.3) | copy-done | bytes 536
  3.2 23.1 %all_gather.3 = bf16[2,2048]{1,0:T(2,128)(2,1)S(1)} all-gather(bf16[2,128]{1,0:T(2,128)(2,1)S(1)} %copy-done.3), channel_id=1, replica_groups=mesh['beam'=4,'pulse'=4,'range'=2] {'beam','pulse'}, dimensions={1}, use_global_device_ids=true | all-gather | bytes 8704 | tf_op jit(solution)/shard_map/all_gather | solution.py:121
  26.4 0.6 copy-done.1
  27.3 0.7 %tile.9 = bf16[278656]{0:T(1024)(128)(2,1)S(1)} reshape(bf16[128,2177]{1,0:T(8,128)(2,1)S(1)} %tile.8) | data formatting | bytes 1114624 | tf_op jit(solution)/shard_map/tile | solution.py:41
  28.0 0.6 reshape.119
  28.7 0.7 %tile.21 = bf16[278656]{0:T(1024)(128)(2,1)S(1)} reshape(bf16[128,2177]{1,0:T(8,128)(2,1)S(1)} %tile.20) | data formatting | bytes 1114624 | tf_op jit(solution)/shard_map/tile | solution.py:41
  29.5 0.6 reshape.120
  30.4 4.0 %while.1 = (s32[]{:T(128)}, bf16[2,8,2,2688]{3,2,1,0:T(2,128)(2,1)S(1)}, s32[2,4]{1,0:T(2,128)S(1)}, bf16[2,8,2,2560]{3,1,0,2:T(8,128)(2,1)S(1)}, s32[]{:T(128)}) while((s32[]{:T(128)}, bf16[2,8,2,2688]{3,2,1,0:T(2,128)(2,1)S(1)}, s32[2,4]{1,0:T(2,128)S(1)}, bf16[2,8,2,2560]{3,1,0,2:T(8,128)(2,1)S(1)}, s32[]{:T(128)}) %tuple.43), condition=%wide.while_cond, body=%wide.while_body.sunk | while | flops 2 | bytes 327813 | solution.py:53
  30.4 0.6 fusion.34
  31.0 1.4 %constant_dynamic-slice_fusion.5 = bf16[1,8,2,2560]{3,2,1,0:T(2,128)(2,1)S(1)} fusion(bf16[2,8,2,2688]{3,2,1,0:T(2,128)(2,1)S(1)} %get-tuple-element.115, s32[]{:T(128)} %bitcast.68, s32[]{:T(128)} %bitcast.69), kind=kLoop, calls=%fused_computation.6.clone.1 | loop fusion | bytes 163848 | tf_op jit(solution)/shard_map/vmap()/gather
  32.4 0.6 fusion.34
  33.0 1.4 %constant_dynamic-slice_fusion.5 = bf16[1,8,2,2560]{3,2,1,0:T(2,128)(2,1)S(1)} fusion(bf16[2,8,2,2688]{3,2,1,0:T(2,128)(2,1)S(1)} %get-tuple-element.115, s32[]{:T(128)} %bitcast.68, s32[]{:T(128)} %bitcast.69), kind=kLoop, calls=%fused_computation.6.clone.1 | loop fusion | bytes 163848 | tf_op jit(solution)/shard_map/vmap()/gather
  36.0 4.7 %collective-permute-start.1 = (f32[2,8,104]{2,1,0:T(8,128)S(1)}, f32[2,8,104]{2,1,0:T(8,128)S(1)}, u32[]{:S(2)}, u32[]{:S(2)}) collective-permute-start(f32[2,8,104]{2,1,0:T(8,128)S(1)} %get-tuple-element.67), channel_id=1, source_target_pairs={{0,1},{2,3},{4,5},{6,7},{8,9},{10,11},{12,13},{14,15},{16,17},{18,... | collective-permute-start | bytes 19976 | tf_op jit(solution)/shard_map/ppermute | solution.py:27
  40.7 1.5 %collective-permute-start.2 = (f32[2,8,104]{2,1,0:T(8,128)S(1)}, f32[2,8,104]{2,1,0:T(8,128)S(1)}, u32[]{:S(2)}, u32[]{:S(2)}) collective-permute-start(f32[2,8,104]{2,1,0:T(8,128)S(1)} %get-tuple-element.68), channel_id=1, source_target_pairs={{1,0},{3,2},{5,4},{7,6},{9,8},{11,10},{13,12},{15,14},{17,16},{19,... | collective-permute-start | bytes 19976 | tf_op jit(solution)/shard_map/ppermute | solution.py:29
  42.2 0.6 %copy.55 = bf16[2,8,2,512]{3,2,1,0:T(2,128)(2,1)} copy(bf16[2,8,2,512]{3,1,2,0:T(8,128)(2,1)S(1)} %copy_bitcast_fusion) | data formatting | bytes 65536
  42.8 3.4 %collective-permute-done.2 = f32[2,8,104]{2,1,0:T(8,128)S(1)} collective-permute-done((f32[2,8,104]{2,1,0:T(8,128)S(1)}, f32[2,8,104]{2,1,0:T(8,128)S(1)}, u32[]{:S(2)}, u32[]{:S(2)}) %collective-permute-start.2) | collective-permute-done | bytes 6688 | tf_op jit(solution)/shard_map/ppermute | solution.py:29
  46.3 3.4 %reduce-window.6 = f32[2,8,6,128]{3,1,2,0:T(8,128)S(1)} reduce-window(f32[2,8,6,128]{3,1,2,0:T(8,128)S(1)} %fusion.5, f32[]{:T(128)} %constant.72.clone.1), window={size=1x1x1x128 pad=0_0x0_0x0_0x127_0}, to_apply=%region_0.1 | reduce-window | flops 1560576 | bytes 98308 | tf_op jit(solution)/shard_map/reduce-window
  50.6 2.6 %gather_fusion.3 = f32[2,8,512]{1,0,2:T(2,128)S(1)} fusion(f32[2,8,721]{1,0,2:T(2,128)S(1)} %concatenate.37, s32[2]{0:T(128)S(1)} %get-tuple-element.72), kind=kCustom, calls=%fused_computation.3 | custom fusion | bytes 65560 | tf_op jit(solution)/shard_map/vmap()/gather | solution.py:103
  53.4 2.6 %gather_fusion.2 = f32[2,8,512]{1,0,2:T(2,128)S(1)} fusion(f32[2,8,721]{1,0,2:T(2,128)S(1)} %concatenate.37, s32[2]{0:T(128)S(1)} %get-tuple-element.70), kind=kCustom, calls=%fused_computation.2 | custom fusion | bytes 65560 | tf_op jit(solution)/shard_map/vmap()/gather | solution.py:103
  56.2 2.6 %gather_fusion.1 = f32[2,8,512]{1,0,2:T(2,128)S(1)} fusion(f32[2,8,721]{1,0,2:T(2,128)S(1)} %concatenate.37, s32[2]{0:T(128)S(1)} %get-tuple-element.69), kind=kCustom, calls=%fused_computation.1 | custom fusion | bytes 65560 | tf_op jit(solution)/shard_map/vmap()/gather | solution.py:103
  59.0 2.6 %gather_fusion = f32[2,8,512]{1,0,2:T(2,128)S(1)} fusion(f32[2,8,721]{1,0,2:T(2,128)S(1)} %concatenate.37, s32[2]{0:T(128)S(1)} %get-tuple-element.71), kind=kCustom, calls=%fused_computation | custom fusion | bytes 65560 | tf_op jit(solution)/shard_map/vmap()/gather | solution.py:103
  61.8 0.7 %multiply_divide_fusion = f32[2,8,512]{2,1,0:T(8,128)} fusion(f32[2,8,512]{2,1,0:T(8,128)S(1)} %copy.53, f32[2,8,512]{2,1,0:T(8,128)S(1)} %copy.54, f32[2,8,512]{2,1,0:T(8,128)S(1)} %copy.51, f32[2,8,512]{2,1,0:T(8,128)S(1)} %copy.52, f32[2,512]{1,0:T(2,128)S(1)} %add_convert_fusion, f32[2]{0:T(128)S(1)} %multiply_exponential_fusion, ...), kind=kLoop, calls=%fused_computation.27 | loop fusion | flops 98304 | bytes 200712 | tf_op jit(solution)/shard_map/div | solution.py:117
  (55 shorter events, 4.0 us)
Async XLA Ops:
  0.6 29.5 %collective-permute-start = (bf16[2,8,2,512]{3,2,1,0:T(2,128)(2,1)}, bf16[2,8,2,512]{3,2,1,0:T(2,128)(2,1)S(1)}, u32[]{:S(2)}, u32[]{:S(2)}) collective-permute-start(bf16[2,8,2,512]{3,2,1,0:T(2,128)(2,1)} %param.6), channel_id=1, source_target_pairs={{1,0},{3,2},{5,4},{7,6},{9,8},{11,10},{13,12},{15,14},{17,16},{19,... | collective-permute-start | bytes 98312 | tf_op jit(solution)/shard_map/ppermute | solution.py:16
  1.9 0.7 %copy-start.4 = (s32[2]{0:T(128)S(1)}, s32[2]{0:T(128)}, u32[]{:S(2)}) copy-start(s32[2]{0:T(128)} %param.11) | copy-start | bytes 28
  2.6 0.7 %copy-start.3 = (bf16[2,128]{1,0:T(2,128)(2,1)S(1)}, bf16[2,128]{1,0:T(2,128)(2,1)}, u32[]{:S(2)}) copy-start(bf16[2,128]{1,0:T(2,128)(2,1)} %param.7) | copy-start | bytes 1540
  26.3 0.7 %copy-start.1 = (s32[2]{0:T(128)S(1)}, s32[2]{0:T(128)}, u32[]{:S(2)}) copy-start(s32[2]{0:T(128)} %param.9) | copy-start | bytes 28
  26.3 0.7 %copy-start.2 = (s32[2]{0:T(128)S(1)}, s32[2]{0:T(128)}, u32[]{:S(2)}) copy-start(s32[2]{0:T(128)} %param.8) | copy-start | bytes 28
  29.5 0.8 %copy-start = (bf16[2,8,2,512]{3,2,1,0:T(2,128)(2,1)S(1)}, bf16[2,8,2,512]{3,2,1,0:T(2,128)(2,1)}, u32[]{:S(2)}) copy-start(bf16[2,8,2,512]{3,2,1,0:T(2,128)(2,1)} %param.6) | copy-start | bytes 98308
  36.0 6.2 %copy-start.5 = (s32[2]{0:T(128)S(1)}, s32[2]{0:T(128)}, u32[]{:S(2)}) copy-start(s32[2]{0:T(128)} %param.10) | copy-start | bytes 28
  36.0 6.8 %collective-permute-start.1 = (f32[2,8,104]{2,1,0:T(8,128)S(1)}, f32[2,8,104]{2,1,0:T(8,128)S(1)}, u32[]{:S(2)}, u32[]{:S(2)}) collective-permute-start(f32[2,8,104]{2,1,0:T(8,128)S(1)} %get-tuple-element.67), channel_id=1, source_target_pairs={{0,1},{2,3},{4,5},{6,7},{8,9},{10,11},{12,13},{14,15},{16,17},{18,... | collective-permute-start | bytes 19976 | tf_op jit(solution)/shard_map/ppermute | solution.py:27
  40.7 5.5 %collective-permute-start.2 = (f32[2,8,104]{2,1,0:T(8,128)S(1)}, f32[2,8,104]{2,1,0:T(8,128)S(1)}, u32[]{:S(2)}, u32[]{:S(2)}) collective-permute-start(f32[2,8,104]{2,1,0:T(8,128)S(1)} %get-tuple-element.68), channel_id=1, source_target_pairs={{1,0},{3,2},{5,4},{7,6},{9,8},{11,10},{13,12},{15,14},{17,16},{19,... | collective-permute-start | bytes 19976 | tf_op jit(solution)/shard_map/ppermute | solution.py:29
where the time goes:
time: 62.8 us; the launch traced here: 62.5 us
  blocking collectives  23.1 us (37%)
  local copies, waits for them, and re-layouts  21.7 us (35%)
  starting transfers between devices  7.43 us (12%)
  other arithmetic  4.6 us (7%)
  waiting for transfers between devices  3.4 us (5%)
  matrix products  1.32 us (2%)
  between operations  0.91 us (1%)
    all_gather x1, blocking collectives, body(): whole = lax.all_gather(replica, ('beam', 'pulse'), axis=1, tiled=True)  23.1 us
    gather x8, local copies, waits for them, and re-layouts, window(): return lax.dynamic_slice_in_dim(block, start, length, 1)  11.1 us
    ppermute x1, starting transfers between devices, padded_2(): lax.ppermute(tail, axis, [(i, (i + 1) % count) for i in range(ends)])  4.67 us
    gather x8, local copies, waits for them, and re-layouts  3.94 us
    another operation x4, other arithmetic  3.57 us
    ppermute x1, waiting for transfers between devices, padded_2(): lax.ppermute(head, axis, [((i + 1) % count, i) for i in range(ends)])  3.4 us
    unnamed x16, local copies, waits for them, and re-layouts  3.09 us
    another operation x4, local copies, waits for them, and re-layouts, skewed(): flat = jnp.tile(padded, TILE)[:TILE * width]  1.53 us
  transfers between devices with their start and end apart: 3, of which 1 were waited for; matrix products, arithmetic and copies ran while one was open for 6% of the time, Pallas kernels for 0%

commit v1 on v0

--- a/solution.py
+++ b/solution.py
@@ -118,7 +118,10 @@
 
 
 def body(signal, replica, guard_cells, train_cells, scale_index, offsets):
-    whole = lax.all_gather(replica, ("beam", "pulse"), axis=1, tiled=True)
+    n_dev = lax.axis_size(("beam", "pulse"))
+    parts = jnp.stack([replica for _ in range(n_dev)])
+    parts = lax.all_to_all(parts, ("beam", "pulse"), split_axis=0, concat_axis=0)
+    whole = jnp.concatenate(parts, axis=1)
     panel_real, panel_imag = panels(whole)
     gate_count = signal.shape[3]
     margin = GUARD_MAX + TRAIN_MAX

time: 62.8 us -> 50.3 us (0.80)
  blocking collectives: 23.1 us -> 0 us
  starting transfers between devices: 7.43 us -> 13.7 us
  waiting for transfers between devices: 3.4 us -> 6.91 us
  local copies, waits for them, and re-layouts: 21.7 us -> 22.4 us
    all_gather x1 -> x0, blocking collectives: 23.1 us -> none  [body(): whole = lax.all_gather(replica, ('beam', 'pulse'), axis=1, tiled=True)]
    all_to_all x0 -> x1, starting transfers between devices: none -> 7.39 us  [body(): lax.all_to_all(parts, ('beam', 'pulse'), split_axis=0, concat_axis=0)]
    all_to_all x0 -> x1, waiting for transfers between devices: none -> 3.5 us  [body(): lax.all_to_all(parts, ('beam', 'pulse'), split_axis=0, concat_axis=0)]
    another operation x4 -> x5, local copies, waits for them, and re-layouts: 0.22 us -> 1.48 us  [the longest x1 1.26 us: body(): parts = jnp.stack([replica for _ in range(n_dev)])]
    ppermute x1, starting transfers between devices: 4.67 us -> 3.55 us  [padded_2(): lax.ppermute(tail, axis, [(i, (i + 1) % count) for i in range(ends)])]
    unnamed x16 -> x14, local copies, waits for them, and re-layouts: 3.09 us -> 2.49 us
  transfers between devices with their start and end apart: 3 -> 4, of which waited for: 1 -> 2; matrix products, arithmetic and copies ran while one was open for 6% -> 7% of each run, Pallas kernels for 0% -> 0%
where the time goes in v1:
time: 50.3 us; the launch traced here: 49.9 us
  local copies, waits for them, and re-layouts  22.4 us (45%)
  starting transfers between devices  13.7 us (27%)
  waiting for transfers between devices  6.91 us (14%)
  other arithmetic  4.6 us (9%)
  matrix products  1.32 us (3%)
  between operations  0.92 us (2%)
    gather x8, local copies, waits for them, and re-layouts, window(): return lax.dynamic_slice_in_dim(block, start, length, 1)  11.1 us
    all_to_all x1, starting transfers between devices, body(): lax.all_to_all(parts, ('beam', 'pulse'), split_axis=0, concat_axis=0)  7.39 us
    gather x8, local copies, waits for them, and re-layouts  4.09 us
    another operation x4, other arithmetic  3.57 us
    ppermute x1, starting transfers between devices, padded_2(): lax.ppermute(tail, axis, [(i, (i + 1) % count) for i in range(ends)])  3.55 us
    all_to_all x1, waiting for transfers between devices, body(): lax.all_to_all(parts, ('beam', 'pulse'), split_axis=0, concat_axis=0)  3.5 us
    ppermute x1, waiting for transfers between devices, padded_2(): lax.ppermute(head, axis, [((i + 1) % count, i) for i in range(ends)])  3.4 us
    unnamed x14, local copies, waits for them, and re-layouts  2.49 us
  transfers between devices with their start and end apart: 4, of which 2 were waited for; matrix products, arithmetic and copies ran while one was open for 7% of the time, Pallas kernels for 0%

profile of v1, /device:TPU:0, one launch (start us, length us, event | category | flops | bytes accessed | tf_op | source)
XLA Modules:
  0.0 49.9 jit_solution(46706849598493653)
XLA Ops:
  0.6 1.3 %stack.56 = bf16[16,2,128]{2,1,0:T(2,128)(2,1)} broadcast(bf16[2,128]{1,0:T(2,128)(2,1)} %param.7), dimensions={1,2} | broadcast | bytes 8704 | tf_op jit(solution)/shard_map/stack | solution.py:122
  1.9 7.4 %all-to-all-start = ((bf16[16,2,128]{2,1,0:T(2,128)(2,1)}), bf16[16,2,128]{2,1,0:T(2,128)(2,1)S(1)}, u32[]{:S(2)}, u32[]{:S(2)}) async-start(bf16[16,2,128]{2,1,0:T(2,128)(2,1)} %stack.56), calls=%async_computation | async-start | bytes 16384 | tf_op jit(solution)/shard_map/all_to_all | solution.py:123
  9.3 1.3 %collective-permute-start = (bf16[2,8,2,512]{3,2,1,0:T(2,128)(2,1)}, bf16[2,8,2,512]{3,2,1,0:T(2,128)(2,1)S(1)}, u32[]{:S(2)}, u32[]{:S(2)}) collective-permute-start(bf16[2,8,2,512]{3,2,1,0:T(2,128)(2,1)} %param.6), channel_id=1, source_target_pairs={{1,0},{3,2},{5,4},{7,6},{9,8},{11,10},{13,12},{15,14},{17,16},{19,... | collective-permute-start | bytes 98312 | tf_op jit(solution)/shard_map/ppermute | solution.py:16
  10.6 0.6 %copy-done.3 = s32[2]{0:T(128)S(1)} copy-done((s32[2]{0:T(128)S(1)}, s32[2]{0:T(128)}, u32[]{:S(2)}) %copy-start.3) | copy-done | bytes 32
  11.3 0.6 %copy-done.1 = s32[2]{0:T(128)S(1)} copy-done((s32[2]{0:T(128)S(1)}, s32[2]{0:T(128)}, u32[]{:S(2)}) %copy-start.1) | copy-done | bytes 32
  12.1 3.5 %all-to-all-done = bf16[16,2,128]{2,1,0:T(2,128)(2,1)S(1)} async-done(((bf16[16,2,128]{2,1,0:T(2,128)(2,1)}), bf16[16,2,128]{2,1,0:T(2,128)(2,1)S(1)}, u32[]{:S(2)}, u32[]{:S(2)}) %all-to-all-start) | async-done | bytes 8224 | tf_op jit(solution)/shard_map/all_to_all | solution.py:123
  15.7 0.7 %tile.9 = bf16[278656]{0:T(1024)(128)(2,1)S(1)} reshape(bf16[128,2177]{1,0:T(8,128)(2,1)S(1)} %tile.8) | data formatting | bytes 1114624 | tf_op jit(solution)/shard_map/tile | solution.py:41
  16.5 0.6 %reshape.130 = bf16[128,2176]{1,0:T(8,128)(2,1)S(1)} reshape(bf16[278528]{0:T(1024)(128)(2,1)S(1)} %slice.100) | data formatting | bytes 1114112 | tf_op jit(solution)/shard_map/reshape | solution.py:42
  17.2 0.7 %tile.21 = bf16[278656]{0:T(1024)(128)(2,1)S(1)} reshape(bf16[128,2177]{1,0:T(8,128)(2,1)S(1)} %tile.20) | data formatting | bytes 1114624 | tf_op jit(solution)/shard_map/tile | solution.py:41
  17.9 0.6 %reshape.131 = bf16[128,2176]{1,0:T(8,128)(2,1)S(1)} reshape(bf16[278528]{0:T(1024)(128)(2,1)S(1)} %slice.103) | data formatting | bytes 1114112 | tf_op jit(solution)/shard_map/reshape | solution.py:42
  18.8 4.2 %while.1 = (s32[]{:T(128)}, bf16[2,8,2,2688]{3,2,1,0:T(2,128)(2,1)S(1)}, s32[2,4]{1,0:T(2,128)S(1)}, bf16[2,8,2,2560]{3,1,0,2:T(8,128)(2,1)S(1)}, s32[]{:T(128)}) while((s32[]{:T(128)}, bf16[2,8,2,2688]{3,2,1,0:T(2,128)(2,1)S(1)}, s32[2,4]{1,0:T(2,128)S(1)}, bf16[2,8,2,2560]{3,1,0,2:T(8,128)(2,1)S(1)}, s32[]{:T(128)}) %tuple.43), condition=%wide.while_cond, body=%wide.while_body.sunk | while | flops 2 | bytes 327813 | solution.py:53
  18.8 0.6 %fusion.34 = (s32[1,1]{1,0:T(1,128)}, s32[1,1]{1,0:T(1,128)}) fusion(s32[1,4]{1,0:T(1,128)S(1)} %constant_dynamic-slice_fusion.4), kind=kLoop, calls=%fused_computation.60.clone.1 | loop fusion | bytes 16 | tf_op jit(solution)/shard_map/vmap()/gather
  19.4 1.4 %constant_dynamic-slice_fusion.5 = bf16[1,8,2,2560]{3,2,1,0:T(2,128)(2,1)S(1)} fusion(bf16[2,8,2,2688]{3,2,1,0:T(2,128)(2,1)S(1)} %get-tuple-element.115, s32[]{:T(128)} %bitcast.75, s32[]{:T(128)} %bitcast.76), kind=kLoop, calls=%fused_computation.6.clone.1 | loop fusion | bytes 163848 | tf_op jit(solution)/shard_map/vmap()/gather
  21.5 1.4 %constant_dynamic-slice_fusion.5 = bf16[1,8,2,2560]{3,2,1,0:T(2,128)(2,1)S(1)} fusion(bf16[2,8,2,2688]{3,2,1,0:T(2,128)(2,1)S(1)} %get-tuple-element.115, s32[]{:T(128)} %bitcast.75, s32[]{:T(128)} %bitcast.76), kind=kLoop, calls=%fused_computation.6.clone.1 | loop fusion | bytes 163848 | tf_op jit(solution)/shard_map/vmap()/gather
  24.6 3.5 %collective-permute-start.1 = (f32[2,8,104]{2,1,0:T(8,128)S(1)}, f32[2,8,104]{2,1,0:T(8,128)S(1)}, u32[]{:S(2)}, u32[]{:S(2)}) collective-permute-start(f32[2,8,104]{2,1,0:T(8,128)S(1)} %get-tuple-element.65), channel_id=1, source_target_pairs={{0,1},{2,3},{4,5},{6,7},{8,9},{10,11},{12,13},{14,15},{16,17},{18,... | collective-permute-start | bytes 19976 | tf_op jit(solution)/shard_map/ppermute | solution.py:27
  28.1 1.5 %collective-permute-start.2 = (f32[2,8,104]{2,1,0:T(8,128)S(1)}, f32[2,8,104]{2,1,0:T(8,128)S(1)}, u32[]{:S(2)}, u32[]{:S(2)}) collective-permute-start(f32[2,8,104]{2,1,0:T(8,128)S(1)} %get-tuple-element.66), channel_id=1, source_target_pairs={{1,0},{3,2},{5,4},{7,6},{9,8},{11,10},{13,12},{15,14},{17,16},{19,... | collective-permute-start | bytes 19976 | tf_op jit(solution)/shard_map/ppermute | solution.py:29
  29.7 0.6 %copy.57 = bf16[2,8,2,512]{3,2,1,0:T(2,128)(2,1)} copy(bf16[2,8,2,512]{3,1,2,0:T(8,128)(2,1)S(1)} %copy_bitcast_fusion) | data formatting | bytes 65536
  30.3 3.4 %collective-permute-done.2 = f32[2,8,104]{2,1,0:T(8,128)S(1)} collective-permute-done((f32[2,8,104]{2,1,0:T(8,128)S(1)}, f32[2,8,104]{2,1,0:T(8,128)S(1)}, u32[]{:S(2)}, u32[]{:S(2)}) %collective-permute-start.2) | collective-permute-done | bytes 6688 | tf_op jit(solution)/shard_map/ppermute | solution.py:29
  33.8 3.4 %reduce-window.6 = f32[2,8,6,128]{3,1,2,0:T(8,128)S(1)} reduce-window(f32[2,8,6,128]{3,1,2,0:T(8,128)S(1)} %fusion.5, f32[]{:T(128)} %constant.72.clone.1), window={size=1x1x1x128 pad=0_0x0_0x0_0x127_0}, to_apply=%region_0.1 | reduce-window | flops 1560576 | bytes 98308 | tf_op jit(solution)/shard_map/reduce-window
  38.1 2.6 %gather_fusion.3 = f32[2,8,512]{1,0,2:T(2,128)S(1)} fusion(f32[2,8,721]{1,0,2:T(2,128)S(1)} %concatenate.37, s32[2]{0:T(128)S(1)} %get-tuple-element.72), kind=kCustom, calls=%fused_computation.3 | custom fusion | bytes 65560 | tf_op jit(solution)/shard_map/vmap()/gather | solution.py:103
  40.9 2.6 %gather_fusion.2 = f32[2,8,512]{1,0,2:T(2,128)S(1)} fusion(f32[2,8,721]{1,0,2:T(2,128)S(1)} %concatenate.37, s32[2]{0:T(128)S(1)} %get-tuple-element.70), kind=kCustom, calls=%fused_computation.2 | custom fusion | bytes 65560 | tf_op jit(solution)/shard_map/vmap()/gather | solution.py:103
  43.7 2.6 %gather_fusion.1 = f32[2,8,512]{1,0,2:T(2,128)S(1)} fusion(f32[2,8,721]{1,0,2:T(2,128)S(1)} %concatenate.37, s32[2]{0:T(128)S(1)} %get-tuple-element.69), kind=kCustom, calls=%fused_computation.1 | custom fusion | bytes 65560 | tf_op jit(solution)/shard_map/vmap()/gather | solution.py:103
  46.4 2.6 %gather_fusion = f32[2,8,512]{1,0,2:T(2,128)S(1)} fusion(f32[2,8,721]{1,0,2:T(2,128)S(1)} %concatenate.37, s32[2]{0:T(128)S(1)} %get-tuple-element.71), kind=kCustom, calls=%fused_computation | custom fusion | bytes 65560 | tf_op jit(solution)/shard_map/vmap()/gather | solution.py:103
  49.2 0.7 %multiply_divide_fusion = f32[2,8,512]{2,1,0:T(8,128)} fusion(f32[2,8,512]{2,1,0:T(8,128)S(1)} %copy.55, f32[2,8,512]{2,1,0:T(8,128)S(1)} %copy.56, f32[2,8,512]{2,1,0:T(8,128)S(1)} %copy.53, f32[2,8,512]{2,1,0:T(8,128)S(1)} %copy.54, f32[2,512]{1,0:T(2,128)S(1)} %add_convert_fusion, f32[2]{0:T(128)S(1)} %multiply_exponential_fusion, ...), kind=kLoop, calls=%fused_computation.27 | loop fusion | flops 98304 | bytes 200712 | tf_op jit(solution)/shard_map/div | solution.py:117
  (56 shorter events, 4.5 us)
Async XLA Ops:
  1.9 13.8 %all-to-all-start = ((bf16[16,2,128]{2,1,0:T(2,128)(2,1)}), bf16[16,2,128]{2,1,0:T(2,128)(2,1)S(1)}, u32[]{:S(2)}, u32[]{:S(2)}) async-start(bf16[16,2,128]{2,1,0:T(2,128)(2,1)} %stack.56), calls=%async_computation | async-start | bytes 16384 | tf_op jit(solution)/shard_map/all_to_all | solution.py:123
  9.3 9.3 %collective-permute-start = (bf16[2,8,2,512]{3,2,1,0:T(2,128)(2,1)}, bf16[2,8,2,512]{3,2,1,0:T(2,128)(2,1)S(1)}, u32[]{:S(2)}, u32[]{:S(2)}) collective-permute-start(bf16[2,8,2,512]{3,2,1,0:T(2,128)(2,1)} %param.6), channel_id=1, source_target_pairs={{1,0},{3,2},{5,4},{7,6},{9,8},{11,10},{13,12},{15,14},{17,16},{19,... | collective-permute-start | bytes 98312 | tf_op jit(solution)/shard_map/ppermute | solution.py:16
  10.6 0.7 %copy-start.3 = (s32[2]{0:T(128)S(1)}, s32[2]{0:T(128)}, u32[]{:S(2)}) copy-start(s32[2]{0:T(128)} %param.11) | copy-start | bytes 28
  11.2 0.7 %copy-start.1 = (s32[2]{0:T(128)S(1)}, s32[2]{0:T(128)}, u32[]{:S(2)}) copy-start(s32[2]{0:T(128)} %param.9) | copy-start | bytes 28
  11.2 0.7 %copy-start.2 = (s32[2]{0:T(128)S(1)}, s32[2]{0:T(128)}, u32[]{:S(2)}) copy-start(s32[2]{0:T(128)} %param.8) | copy-start | bytes 28
  17.9 0.8 %copy-start = (bf16[2,8,2,512]{3,2,1,0:T(2,128)(2,1)S(1)}, bf16[2,8,2,512]{3,2,1,0:T(2,128)(2,1)}, u32[]{:S(2)}) copy-start(bf16[2,8,2,512]{3,2,1,0:T(2,128)(2,1)} %param.6) | copy-start | bytes 98308
  24.6 5.0 %copy-start.4 = (s32[2]{0:T(128)S(1)}, s32[2]{0:T(128)}, u32[]{:S(2)}) copy-start(s32[2]{0:T(128)} %param.10) | copy-start | bytes 28
  24.6 5.7 %collective-permute-start.1 = (f32[2,8,104]{2,1,0:T(8,128)S(1)}, f32[2,8,104]{2,1,0:T(8,128)S(1)}, u32[]{:S(2)}, u32[]{:S(2)}) collective-permute-start(f32[2,8,104]{2,1,0:T(8,128)S(1)} %get-tuple-element.65), channel_id=1, source_target_pairs={{0,1},{2,3},{4,5},{6,7},{8,9},{10,11},{12,13},{14,15},{16,17},{18,... | collective-permute-start | bytes 19976 | tf_op jit(solution)/shard_map/ppermute | solution.py:27
  28.1 5.5 %collective-permute-start.2 = (f32[2,8,104]{2,1,0:T(8,128)S(1)}, f32[2,8,104]{2,1,0:T(8,128)S(1)}, u32[]{:S(2)}, u32[]{:S(2)}) collective-permute-start(f32[2,8,104]{2,1,0:T(8,128)S(1)} %get-tuple-element.66), channel_id=1, source_target_pairs={{1,0},{3,2},{5,4},{7,6},{9,8},{11,10},{13,12},{15,14},{17,16},{19,... | collective-permute-start | bytes 19976 | tf_op jit(solution)/shard_map/ppermute | solution.py:29
